TPU v7x, 128 devices: a whole 4x4x4 slice. The times are simulated.
128 devices in a mesh: row: 8 (over z, core), col: 16 (over x, y).
Axes of the slice: x: 4, y: 4, z: 4, core: 2. Of those that a mesh axis runs over, the one named last changes fastest.
Arguments:
- a_blocks: float32 [1024, 8, 256, 256], P(('row', 'col')), may hold values from -0.09375 to 0.09375
- a_live: int32 [1024, 8], P(('row', 'col')), may hold values from 0 to 1, as said below
- p_blocks: float32 [1024, 256, 2, 128], P(('row', 'col')), may hold values from -0.1875 to 0.1875
- p_cols: int32 [1024, 2], P(('row', 'col')), may hold values from 0 to 127, as said below
- ghost_list: int32 [1024, 7], P(('row', 'col')), may hold values from 0 to 7, as said below
- policy: int32 [1024], P(('row', 'col')), may hold values from 0 to 15
- rates: float32 [16, 256], replicated, may hold values from 0.1 to 1
- rhs: float32 [16384, 256], P(('row', 'col')), may hold values from -6 to 6
- guess: float32 [16384, 256], P(('row', 'col')), may hold values from -6 to 6
Outputs:
- coarse: float32 [16384, 8, 16, 128], P('row', None, 'col')
- smoothed: float32 [16384, 256], P(('row', 'col'))
Inputs may be any that keep to these rules, and one draw needn't show every extreme that they name: a_live[i, 0] is 1 for every i. On each device and for each k, the entries ghost_list[d * 8 + s, k] over s = 0 .. 7 are a permutation of 0 .. 7. p_cols[j, m] modulo the number of col devices equals (col index of the device holding block row j + m * 8) modulo that number. The quotient by that number names a mesh row: among the 16 entries of one device at most 2 name the same mesh row, and the device's own mesh row is named exactly 2 times, by at least one entry of each m.
All inputs are finite; a program needn't handle non-finite values.
Results may differ from a plain program's by a relative error of at most 0.0003.
Values sent between devices are 32-bit elements; how exact they have to be, the bound alone decides.
No kernel may reach another device: no remote copies, remote signals or barrier semaphores. Data moves between devices by JAX's collectives and lax.ppermute only.
A program may use at most 192 MiB of HBM per device.

v0:
```python
import jax
import jax.numpy as jnp
from jax import lax
from jax.sharding import PartitionSpec as P

BS = 256
CB = 128
KA = 8
KP = 2
NPOL = 16
damping = 0.7


def from_behind(value, axis, steps):
    count = lax.axis_size(axis)
    pairs = [(source, (source + steps) % count) for source in range(count)]
    return lax.ppermute(value, axis, pairs)


def on_device(a_blocks, a_live, p_blocks, p_cols, ghost_list, policy, rates, rhs, guess):
    highest = lax.Precision.HIGHEST
    row_count = lax.axis_size("row")
    col_count = lax.axis_size("col")
    dev_count = row_count * col_count
    row_here = lax.axis_index("row")
    col_here = lax.axis_index("col")
    local_rows = a_blocks.shape[0]
    own_p = p_blocks.reshape(local_rows, BS, KP * CB)
    send_p = []
    send_c = []
    for offset in range(1, KA):
        picks = ghost_list[:, offset - 1]
        send_p.append(own_p[picks])
        send_c.append(p_cols[picks].astype(jnp.float32))
    incoming_p = [own_p]
    incoming_c = [p_cols]
    for offset in range(1, KA):
        moved_p, moved_c = from_behind((send_p[offset - 1], send_c[offset - 1]), "col", offset)
        incoming_p.append(moved_p)
        incoming_c.append(moved_c.astype(jnp.int32))
    ghost_p = jnp.stack(incoming_p, axis=1)
    ghost_c = jnp.stack(incoming_c, axis=1)
    live = a_live.astype(jnp.float32)
    selector = (policy[:, None] == jnp.arange(NPOL, dtype=jnp.int32)[None, :]).astype(jnp.float32)
    rate_rows = jnp.dot(selector, rates, precision=highest)
    product = jnp.einsum("skab,skbn->skan", a_blocks, ghost_p, precision=highest)
    product = product * live[:, :, None, None]
    product = product.at[:, 0].add(rate_rows[:, :, None] * own_p)
    partial_value = jnp.einsum("sam,skan->skmn", own_p, product, precision=highest)
    partial_value = (
        partial_value.reshape(local_rows, KA, KP, CB, KP, CB)
        .transpose(0, 1, 2, 4, 3, 5)
        .reshape(-1, CB, CB)
    )
    first = jnp.broadcast_to(p_cols[:, None, :, None], (local_rows, KA, KP, KP)).reshape(-1)
    second = jnp.broadcast_to(ghost_c[:, :, None, :], (local_rows, KA, KP, KP)).reshape(-1)
    alive = jnp.broadcast_to(a_live[:, :, None, None] > 0, (local_rows, KA, KP, KP)).reshape(-1)
    owner = first // col_count * col_count + second % col_count
    spot = first % col_count * row_count + second // col_count
    order = jnp.arange(owner.shape[0], dtype=jnp.int32)
    earlier = (
        (owner[None, :] == owner[:, None]) & alive[None, :] & (order[None, :] < order[:, None])
    )
    rank = jnp.sum(earlier.astype(jnp.int32), axis=1)
    row_cap = max(2, -(-(local_rows * KP) // row_count))
    slot_cap = row_cap * max(1, KA * KP // col_count)
    slot = jnp.where(alive, owner * slot_cap + rank, dev_count * slot_cap)
    sent_blocks = jax.ops.segment_sum(partial_value, slot, num_segments=dev_count * slot_cap + 1)[
        :-1
    ]
    sent_spots = jax.ops.segment_sum(
        (spot + 1).astype(jnp.float32), slot, num_segments=dev_count * slot_cap + 1
    )[:-1]
    got_blocks, got_spots = (
        lax.all_to_all(
            sent_blocks.reshape(dev_count, slot_cap, CB, CB),
            ("row", "col"),
            split_axis=0,
            concat_axis=0,
            tiled=True,
        ),
        lax.all_to_all(
            sent_spots.reshape(dev_count, slot_cap),
            ("row", "col"),
            split_axis=0,
            concat_axis=0,
            tiled=True,
        ),
    )
    places = got_spots.reshape(-1).astype(jnp.int32) - 1
    places = jnp.where(places < 0, dev_count, places)
    summed = jax.ops.segment_sum(
        got_blocks.reshape(-1, CB, CB), places, num_segments=dev_count + 1
    )[:-1]
    coarse = (
        summed.reshape(col_count, row_count, CB, CB)
        .transpose(0, 2, 1, 3)
        .reshape(col_count * CB, row_count, 1, CB)
    )
    matrix = coarse.reshape(col_count * CB, row_count * CB)
    own_block = lax.dynamic_slice(matrix, (col_here * CB, row_here * CB), (CB, CB))
    floor_diag = jnp.maximum(jnp.abs(jnp.diagonal(own_block)), 1.0)
    current = guess
    for sweep in range(2):
        gathered = lax.all_gather(current, "row", axis=0, tiled=True)
        applied = lax.psum_scatter(
            jnp.dot(matrix, gathered, precision=highest), "col", scatter_dimension=0, tiled=True
        )
        current = current + damping * (rhs - applied) / floor_diag[:, None]
    return (coarse, current)


def solution(mesh):
    return jax.shard_map(
        on_device,
        mesh=mesh,
        in_specs=(
            P(("row", "col"), None, None, None),
            P(("row", "col"), None),
            P(("row", "col"), None, None, None),
            P(("row", "col"), None),
            P(("row", "col"), None),
            P(("row", "col")),
            P(),
            P(("row", "col"), None),
            P(("row", "col"), None),
        ),
        out_specs=(P("row", None, "col", None), P(("row", "col"), None)),
        check_vma=False,
    )
```

profile of v0, /device:TPU:0, one launch (start us, length us, event | category | flops | bytes accessed | tf_op | source)
XLA Modules:
  0.0 1113.7 jit_solution(12962005515692555085)
XLA Ops:
  7.2 1.2 fusion.9
  9.8 3.4 collective-permute-start.1
  15.0 3.6 collective-permute-start.2
  18.6 2.9 reshape.341
  21.5 2.0 gather_fusion.8
  23.5 2.9 copy.130
  26.5 2.0 gather_fusion.7
  28.5 2.9 copy.129
  31.4 1.6 collective-permute-start.7
  34.1 4.1 copy.128
  38.2 2.0 gather_fusion.9
  40.8 2.0 gather_fusion.10
  43.3 2.0 gather_fusion.11
  45.9 2.0 gather_fusion.12
  48.4 2.1 gather_fusion.13
  50.5 4.1 reshape.490
  54.6 1.8 copy.131
  56.4 3.1 copy.132
  59.5 1.8 copy.133
  61.4 3.0 copy.134
  64.4 1.5 constant_dynamic-update-slice_fusion.8
  65.9 2.9 copy.135
  68.8 1.2 collective-permute-start.3
  70.1 2.7 collective-permute-start.4
  72.9 2.2 collective-permute-start.5
  75.2 47.6 %collective-permute-start.9 = (f32[8,256,256]{1,2,0:T(8,128)}, f32[8,256,256]{1,2,0:T(8,128)}, u32[]{:S(2)}, u32[]{:S(2)}) collective-permute-start(f32[8,256,256]{1,2,0:T(8,128)} %copy.131), channel_id=1, source_target_pairs={{0,3},{1,4},{2,5},{3,6},{4,7},{5,8},{6,9},{7,10},{8,11},{9,12},{10... | collective-permute-start | bytes 6291464 | tf_op jit(solution)/shard_map/ppermute | solution.py:17
  123.9 44.1 %collective-permute-done.6 = f32[8,2]{1,0:T(8,128)S(1)} collective-permute-done((f32[8,2]{1,0:T(8,128)S(1)}, f32[8,2]{1,0:T(8,128)S(1)}, u32[]{:S(2)}, u32[]{:S(2)}) %collective-permute-start.6) | collective-permute-done | bytes 96 | tf_op jit(solution)/shard_map/ppermute | solution.py:17
  168.4 47.3 %collective-permute-start.12 = (f32[8,256,256]{1,2,0:T(8,128)}, f32[8,256,256]{1,2,0:T(8,128)}, u32[]{:S(2)}, u32[]{:S(2)}) collective-permute-start(f32[8,256,256]{1,2,0:T(8,128)} %copy.134), channel_id=1, source_target_pairs={{0,6},{1,7},{2,8},{3,9},{4,10},{5,11},{6,12},{7,13},{8,14},{9,15},... | collective-permute-start | bytes 6291464 | tf_op jit(solution)/shard_map/ppermute | solution.py:17
  216.0 6.1 collective-permute-start.13
  222.2 2.3 scatter_custom_fusion
  224.5 0.8 all_to_all.9
  225.3 7.6 all-to-all-start
  232.9 3.0 bitcast_dynamic-update-slice_fusion.6
  235.9 3.0 bitcast_dynamic-update-slice_fusion.5
  238.9 3.0 bitcast_dynamic-update-slice_fusion.4
  241.9 3.0 bitcast_dynamic-update-slice_fusion.3
  244.9 16.2 %collective-permute-done.11 = f32[8,256,256]{1,2,0:T(8,128)} collective-permute-done((f32[8,256,256]{1,2,0:T(8,128)}, f32[8,256,256]{1,2,0:T(8,128)}, u32[]{:S(2)}, u32[]{:S(2)}) %collective-permute-start.11) | collective-permute-done | bytes 2097184 | tf_op jit(solution)/shard_map/ppermute | solution.py:17
  261.1 3.0 bitcast_dynamic-update-slice_fusion.2
  264.1 88.1 %collective-permute-done.12 = f32[8,256,256]{1,2,0:T(8,128)} collective-permute-done((f32[8,256,256]{1,2,0:T(8,128)}, f32[8,256,256]{1,2,0:T(8,128)}, u32[]{:S(2)}, u32[]{:S(2)}) %collective-permute-start.12) | collective-permute-done | bytes 2097184 | tf_op jit(solution)/shard_map/ppermute | solution.py:17
  352.2 3.0 bitcast_dynamic-update-slice_fusion.1
  355.1 3.0 bitcast_dynamic-update-slice_fusion
  358.2 43.2 %multiply_bitcast_fusion = f32[8,8,256,256]{2,3,1,0:T(8,128)} fusion(f32[8,8,256,256]{2,3,1,0:T(8,128)} %bitcast_dynamic-update-slice_fusion, f32[8,8,256,256]{3,2,1,0:T(8,128)} %param.11, f32[8,8]{1,0:T(8,128)S(1)} %convert_element_type.80), kind=kOutput, calls=%fused_computation.18 | convolution fusion | flops 12889096192 | bytes 50331904 | tf_op jit(solution)/shard_map/skab,skbn->skan/dot_general | solution.py:46
  401.4 3.3 fusion
  404.7 21.4 %convolution_bitcast_fusion = f32[8,8,256,256]{2,3,1,0:T(8,128)} fusion(f32[8,8,256,256]{2,3,1,0:T(8,128)} %fusion, f32[8,256,256,1]{2,1,0,3:T(8,128)S(1)} %copy-done.3), kind=kOutput, calls=%fused_computation.19 | convolution fusion | flops 12884901888 | bytes 35651584 | tf_op jit(solution)/shard_map/sam,skan->skmn/dot_general | solution.py:49
  426.1 20.8 %reshape.342 = f32[8,8,2,128,2,128]{3,2,5,4,1,0:T(2,128)} reshape(f32[8,8,256,256]{2,3,1,0:T(8,128)} %convolution_bitcast_fusion) | data formatting | bytes 33554432 | tf_op jit(solution)/shard_map/reshape | solution.py:51
  446.9 25.0 %copy.136 = f32[8,8,2,128,2,128]{5,3,4,2,1,0:T(8,128)} copy(f32[8,8,2,128,2,128]{3,2,5,4,1,0:T(2,128)} %reshape.342) | data formatting | bytes 33554432 | tf_op jit(solution)/shard_map/reshape | solution.py:51
  471.9 7.9 broadcast_in_dim.27
  479.7 51.5 %scatter_fusion = f32[257,128,128]{2,1,0:T(8,128)} fusion(f32[257,128,128]{2,1,0:T(8,128)} %broadcast_in_dim.27, s32[256]{0:T(256)S(1)} %bitcast.83, f32[256,128,128]{2,1,0:T(8,128)} %bitcast.77), kind=kCustom, calls=%fused_computation.16 | custom fusion | flops 4194304 | bytes 50332672 | tf_op jit(solution)/shard_map/scatter-add | solution.py:68
  531.3 11.6 %slice.99 = f32[256,128,128]{2,1,0:T(8,128)} slice(f32[257,128,128]{2,1,0:T(8,128)} %scatter_fusion), slice={[0:256], [0:128], [0:128]} | slice | bytes 33554432 | tf_op jit(solution)/shard_map/slice | solution.py:68
  542.9 50.5 %all-to-all-start.1 = ((f32[128,2,128,128]{3,2,1,0:T(8,128)}), f32[128,2,128,128]{3,2,1,0:T(8,128)}, u32[]{:S(2)}, u32[]{:S(2)}) async-start(f32[128,2,128,128]{3,2,1,0:T(8,128)} %bitcast.76), calls=%async_computation.1 | async-start | bytes 33554432 | tf_op jit(solution)/shard_map/all_to_all | solution.py:75
  595.0 237.9 %all-to-all-done.1 = f32[128,2,128,128]{3,2,1,0:T(8,128)} async-done(((f32[128,2,128,128]{3,2,1,0:T(8,128)}), f32[128,2,128,128]{3,2,1,0:T(8,128)}, u32[]{:S(2)}, u32[]{:S(2)}) %all-to-all-start.1) | async-done | bytes 16777248 | tf_op jit(solution)/shard_map/all_to_all | solution.py:75
  832.9 4.3 broadcast_in_dim.20
  837.3 51.8 %scatter_fusion.1 = f32[129,128,128]{2,1,0:T(8,128)} fusion(f32[129,128,128]{2,1,0:T(8,128)} %broadcast_in_dim.20, s32[256]{0:T(256)S(1)} %bitcast.84, f32[256,128,128]{2,1,0:T(8,128)} %bitcast.26), kind=kCustom, calls=%fused_computation.17 | custom fusion | flops 4194304 | bytes 50332672 | tf_op jit(solution)/shard_map/scatter-add | solution.py:92
  889.1 4.0 slice.100
  893.0 9.9 copy.137
  903.0 11.6 %fusion.20 = f32[2048,256]{1,0:T(8,128)} fusion(f32[1024,256]{1,0:T(8,128)} %all-gather.3.cloned.1.call-done, f32[256,8,8,128]{3,2,1,0:T(8,128)} %bitcast.72), kind=kOutput, calls=%fused_computation.105 | convolution fusion | flops 6442450944 | bytes 11534336 | tf_op jit(solution)/shard_map/dot_general | solution.py:107
  914.7 5.5 copy.145
  920.2 1.2 gather_fusion.14
  921.5 72.0 %reduce-scatter.3.cloned.1.call-done = f32[128,256]{1,0:T(8,128)} async-done(((f32[2048,256]{1,0:T(8,128)}), f32[128,256]{1,0:T(8,128)}) %reduce-scatter.3.cloned.1.call-update) | async-done | bytes 131088 | tf_op jit(solution)/shard_map/reduce_scatter | solution.py:106
  993.5 1.7 divide_add_fusion.1
  995.2 23.5 %all-gather.5.cloned.1.call-done = f32[1024,256]{1,0:T(8,128)} async-done(((f32[128,256]{1,0:T(8,128)}), f32[1024,256]{1,0:T(8,128)}) %all-gather.5.cloned.1.call-update) | async-done | bytes 1048592 | tf_op jit(solution)/shard_map/all_gather | solution.py:105
  1018.7 11.5 %fusion.19 = f32[2048,256]{1,0:T(8,128)} fusion(f32[1024,256]{1,0:T(8,128)} %all-gather.5.cloned.1.call-done, f32[256,8,8,128]{3,2,1,0:T(8,128)} %bitcast.74), kind=kOutput, calls=%fused_computation.104 | convolution fusion | flops 6442450944 | bytes 11534336 | tf_op jit(solution)/shard_map/dot_general | solution.py:107
  1030.2 75.1 %reduce-scatter.5.cloned.1.call-done = f32[128,256]{1,0:T(8,128)} async-done(((f32[2048,256]{1,0:T(8,128)}), f32[128,256]{1,0:T(8,128)}) %reduce-scatter.5.cloned.1.call-update) | async-done | bytes 131088 | tf_op jit(solution)/shard_map/reduce_scatter | solution.py:106
  1105.3 1.6 divide_add_fusion
  (114 shorter events, 10.4 us)
Async XLA Ops:
  7.2 25.8 %copy-start = (f32[16,256]{1,0:T(8,128)S(1)}, f32[16,256]{1,0:T(8,128)}, u32[]{:S(2)}) copy-start(f32[16,256]{1,0:T(8,128)} %param.17) | copy-start | bytes 49156
  9.8 59.1 %collective-permute-start.1 = (f32[8,2]{1,0:T(8,128)S(1)}, f32[8,2]{1,0:T(8,128)S(1)}, u32[]{:S(2)}, u32[]{:S(2)}) collective-permute-start(f32[8,2]{1,0:T(8,128)S(1)} %convert_element_type.65), channel_id=1, source_target_pairs={{0,2},{1,3},{2,4},{3,5},{4,6},{5,7},{6,8},{7,9},{8,10},{9,11},{10,... | collective-permute-start | bytes 200 | tf_op jit(solution)/shard_map/ppermute | solution.py:17
  13.7 56.4 %collective-permute-start = (f32[8,2]{1,0:T(8,128)S(1)}, f32[8,2]{1,0:T(8,128)S(1)}, u32[]{:S(2)}, u32[]{:S(2)}) collective-permute-start(f32[8,2]{1,0:T(8,128)S(1)} %convert_element_type.63), channel_id=1, source_target_pairs={{0,1},{1,2},{2,3},{3,4},{4,5},{5,6},{6,7},{7,8},{8,9},{9,10},{10,1... | collective-permute-start | bytes 200 | tf_op jit(solution)/shard_map/ppermute | solution.py:17
  15.0 57.9 %collective-permute-start.2 = (f32[8,2]{1,0:T(8,128)S(1)}, f32[8,2]{1,0:T(8,128)S(1)}, u32[]{:S(2)}, u32[]{:S(2)}) collective-permute-start(f32[8,2]{1,0:T(8,128)S(1)} %convert_element_type.67), channel_id=1, source_target_pairs={{0,3},{1,4},{2,5},{3,6},{4,7},{5,8},{6,9},{7,10},{8,11},{9,12},{10... | collective-permute-start | bytes 200 | tf_op jit(solution)/shard_map/ppermute | solution.py:17
  26.4 141.9 %collective-permute-start.8 = (f32[8,256,256]{1,2,0:T(8,128)}, f32[8,256,256]{1,2,0:T(8,128)}, u32[]{:S(2)}, u32[]{:S(2)}) collective-permute-start(f32[8,256,256]{1,2,0:T(8,128)} %copy.130), channel_id=1, source_target_pairs={{0,2},{1,3},{2,4},{3,5},{4,6},{5,7},{6,8},{7,9},{8,10},{9,11},{10,... | collective-permute-start | bytes 6291464 | tf_op jit(solution)/shard_map/ppermute | solution.py:17
  28.5 4.5 copy-start.10
  28.5 4.5 copy-start.9
  28.5 4.5 copy-start.11
  31.4 184.6 %collective-permute-start.7 = (f32[8,256,256]{1,2,0:T(8,128)}, f32[8,256,256]{1,2,0:T(8,128)}, u32[]{:S(2)}, u32[]{:S(2)}) collective-permute-start(f32[8,256,256]{1,2,0:T(8,128)} %copy.129), channel_id=1, source_target_pairs={{0,1},{1,2},{2,3},{3,4},{4,5},{5,6},{6,7},{7,8},{8,9},{9,10},{10,1... | collective-permute-start | bytes 6291464 | tf_op jit(solution)/shard_map/ppermute | solution.py:17
  50.5 4.1 copy-start.4
  56.4 3.1 copy-start.5
  61.4 3.0 copy-start.2
  68.8 6.4 collective-permute-start.3
  70.1 52.7 %collective-permute-start.4 = (f32[8,2]{1,0:T(8,128)S(1)}, f32[8,2]{1,0:T(8,128)S(1)}, u32[]{:S(2)}, u32[]{:S(2)}) collective-permute-start(f32[8,2]{1,0:T(8,128)S(1)} %convert_element_type.71), channel_id=1, source_target_pairs={{0,5},{1,6},{2,7},{3,8},{4,9},{5,10},{6,11},{7,12},{8,13},{9,14},{... | collective-permute-start | bytes 200 | tf_op jit(solution)/shard_map/ppermute | solution.py:17
  72.9 50.3 %collective-permute-start.5 = (f32[8,2]{1,0:T(8,128)S(1)}, f32[8,2]{1,0:T(8,128)S(1)}, u32[]{:S(2)}, u32[]{:S(2)}) collective-permute-start(f32[8,2]{1,0:T(8,128)S(1)} %convert_element_type.73), channel_id=1, source_target_pairs={{0,6},{1,7},{2,8},{3,9},{4,10},{5,11},{6,12},{7,13},{8,14},{9,15},... | collective-permute-start | bytes 200 | tf_op jit(solution)/shard_map/ppermute | solution.py:17
  75.2 163.7 %collective-permute-start.9 = (f32[8,256,256]{1,2,0:T(8,128)}, f32[8,256,256]{1,2,0:T(8,128)}, u32[]{:S(2)}, u32[]{:S(2)}) collective-permute-start(f32[8,256,256]{1,2,0:T(8,128)} %copy.131), channel_id=1, source_target_pairs={{0,3},{1,4},{2,5},{3,6},{4,7},{5,8},{6,9},{7,10},{8,11},{9,12},{10... | collective-permute-start | bytes 6291464 | tf_op jit(solution)/shard_map/ppermute | solution.py:17
  122.8 119.1 %collective-permute-start.10 = (f32[8,256,256]{1,2,0:T(8,128)}, f32[8,256,256]{1,2,0:T(8,128)}, u32[]{:S(2)}, u32[]{:S(2)}) collective-permute-start(f32[8,256,256]{1,2,0:T(8,128)} %copy.132), channel_id=1, source_target_pairs={{0,4},{1,5},{2,6},{3,7},{4,8},{5,9},{6,10},{7,11},{8,12},{9,13},{1... | collective-permute-start | bytes 6291464 | tf_op jit(solution)/shard_map/ppermute | solution.py:17
  123.2 44.8 %collective-permute-start.6 = (f32[8,2]{1,0:T(8,128)S(1)}, f32[8,2]{1,0:T(8,128)S(1)}, u32[]{:S(2)}, u32[]{:S(2)}) collective-permute-start(f32[8,2]{1,0:T(8,128)S(1)} %convert_element_type.75), channel_id=1, source_target_pairs={{0,7},{1,8},{2,9},{3,10},{4,11},{5,12},{6,13},{7,14},{8,15},{9,0},... | collective-permute-start | bytes 200 | tf_op jit(solution)/shard_map/ppermute | solution.py:17
  167.9 93.1 %collective-permute-start.11 = (f32[8,256,256]{1,2,0:T(8,128)}, f32[8,256,256]{1,2,0:T(8,128)}, u32[]{:S(2)}, u32[]{:S(2)}) collective-permute-start(f32[8,256,256]{1,2,0:T(8,128)} %copy.133), channel_id=1, source_target_pairs={{0,5},{1,6},{2,7},{3,8},{4,9},{5,10},{6,11},{7,12},{8,13},{9,14},{... | collective-permute-start | bytes 6291464 | tf_op jit(solution)/shard_map/ppermute | solution.py:17
  168.4 183.8 %collective-permute-start.12 = (f32[8,256,256]{1,2,0:T(8,128)}, f32[8,256,256]{1,2,0:T(8,128)}, u32[]{:S(2)}, u32[]{:S(2)}) collective-permute-start(f32[8,256,256]{1,2,0:T(8,128)} %copy.134), channel_id=1, source_target_pairs={{0,6},{1,7},{2,8},{3,9},{4,10},{5,11},{6,12},{7,13},{8,14},{9,15},... | collective-permute-start | bytes 6291464 | tf_op jit(solution)/shard_map/ppermute | solution.py:17
  216.0 139.1 %collective-permute-start.13 = (f32[8,256,256]{1,2,0:T(8,128)}, f32[8,256,256]{1,2,0:T(8,128)}, u32[]{:S(2)}, u32[]{:S(2)}) collective-permute-start(f32[8,256,256]{1,2,0:T(8,128)} %copy.135), channel_id=1, source_target_pairs={{0,7},{1,8},{2,9},{3,10},{4,11},{5,12},{6,13},{7,14},{8,15},{9,0},... | collective-permute-start | bytes 6291464 | tf_op jit(solution)/shard_map/ppermute | solution.py:17
  225.3 317.7 %all-to-all-start = ((f32[128,1,2]{2,1,0:T(1,128)}), f32[128,1,2]{2,1,0:T(1,128)S(1)}, u32[]{:S(2)}, u32[]{:S(2)}) async-start(f32[128,1,2]{2,1,0:T(1,128)} %bitcast.10), calls=%async_computation | async-start | bytes 131072 | tf_op jit(solution)/shard_map/all_to_all | solution.py:82
  401.4 3.3 copy-start.3
  542.9 290.0 %all-to-all-start.1 = ((f32[128,2,128,128]{3,2,1,0:T(8,128)}), f32[128,2,128,128]{3,2,1,0:T(8,128)}, u32[]{:S(2)}, u32[]{:S(2)}) async-start(f32[128,2,128,128]{3,2,1,0:T(8,128)} %bitcast.76), calls=%async_computation.1 | async-start | bytes 33554432 | tf_op jit(solution)/shard_map/all_to_all | solution.py:75
  593.5 309.5 %all-gather.3.cloned.1.call-start = ((), (), s32[]{:S(2)}) async-start(), calls=%async_computation.4 | async-start | bytes 1179648 | tf_op jit(solution)/shard_map/all_gather | solution.py:105
  594.2 399.3 %reduce-scatter.3.cloned.1.call-start = ((), (), s32[]{:S(2)}) async-start(), calls=%async_computation.5 | async-start | bytes 2228224 | tf_op jit(solution)/shard_map/reduce_scatter | solution.py:106
  914.6 104.1 %all-gather.5.cloned.1.call-start = ((), (), s32[]{:S(2)}) async-start(), calls=%async_computation.6 | async-start | bytes 1179648 | tf_op jit(solution)/shard_map/all_gather | solution.py:105
  914.7 78.8 %copy-start.7 = (f32[128,256]{1,0:T(8,128)S(1)}, f32[128,256]{1,0:T(8,128)}, u32[]{:S(2)}) copy-start(f32[128,256]{1,0:T(8,128)} %param.18) | copy-start | bytes 393220
  914.7 78.8 %copy-start.8 = (f32[128,256]{1,0:T(8,128)S(1)}, f32[128,256]{1,0:T(8,128)}, u32[]{:S(2)}) copy-start(f32[128,256]{1,0:T(8,128)} %param.19) | copy-start | bytes 393220
  995.2 110.1 %reduce-scatter.5.cloned.1.call-start = ((), (), s32[]{:S(2)}) async-start(), calls=%async_computation.7 | async-start | bytes 2228224 | tf_op jit(solution)/shard_map/reduce_scatter | solution.py:106
  1018.7 88.3 %copy-start.1 = (f32[16,256]{1,0:T(8,128)S(1)}, f32[16,256]{1,0:T(8,128)}, u32[]{:S(2)}) copy-start(f32[16,256]{1,0:T(8,128)} %param.17) | copy-start | bytes 49156
  1030.2 75.2 %copy-start.6 = (f32[128,256]{1,0:T(8,128)S(1)}, f32[128,256]{1,0:T(8,128)}, u32[]{:S(2)}) copy-start(f32[128,256]{1,0:T(8,128)} %divide_add_fusion.1) | copy-start | bytes 393220
Sparse Core Ops, SparseCore 0:
  596.0 93.5 all-gather.2
  914.7 78.7 reduce-scatter.2
  995.8 22.8 all-gather.4
  1030.3 74.9 reduce-scatter.4
where the time goes:
time: 1120 us; the launch traced here: 1110 us
  waiting for transfers between devices  558 us (50%)
  starting transfers between devices  176 us (16%)
  local copies, waits for them, and re-layouts  164 us (15%)
  other arithmetic  114 us (10%)
  matrix products  87.9 us (8%)
  between operations  14.3 us (1%)
    all_to_all x1, waiting for transfers between devices, on_device(): lax.all_to_all(sent_blocks.reshape(dev_count, slot_cap, CB, CB), ('row',...  238 us
    ppermute x14, waiting for transfers between devices, from_behind(): return lax.ppermute(value, axis, pairs)  148 us
    reduce_scatter x2, waiting for transfers between devices, on_device(): lax.psum_scatter(jnp.dot(matrix, gathered, precision=highest), 'col', sca...  147 us
    ppermute x14, starting transfers between devices, from_behind(): return lax.ppermute(value, axis, pairs)  117 us
    scatter-add x1, other arithmetic, on_device(): jax.ops.segment_sum(got_blocks.reshape(-1, CB, CB), places, num_segments=...  51.8 us
    scatter-add x1, other arithmetic, on_device(): jax.ops.segment_sum(partial_value, slot, num_segments=dev_count * slot_ca...  51.5 us
    all_to_all x1, starting transfers between devices, on_device(): lax.all_to_all(sent_blocks.reshape(dev_count, slot_cap, CB, CB), ('row',...  50.5 us
    reshape x2, local copies, waits for them, and re-layouts, on_device(): partial_value.reshape(local_rows, KA, KP, CB, KP, CB)  45.7 us
  transfers between devices with their start and end apart: 20, of which 7 were waited for; matrix products, arithmetic and copies ran while one was open for 30% of the time, Pallas kernels for 0%

commit v1 on v0

--- a/solution.py
+++ b/solution.py
@@ -1,3 +1,4 @@
+import functools
 import jax
 import jax.numpy as jnp
 from jax import lax
@@ -9,6 +10,18 @@
 KP = 2
 NPOL = 16
 damping = 0.7
+
+
+def map_views_on_mesh(frame, axis_tag):
+    grid = []
+    for _ in range(jax.lax.axis_size(axis_tag)):
+        grid.append(frame)
+    formed = jnp.stack(grid, axis=0)
+    ready = jax.lax.all_to_all(formed, axis_tag, 0, 0)
+    return jnp.concatenate(ready, axis=0)
+
+
+rates_start = functools.partial(map_views_on_mesh, axis_tag="row")
 
 
 def from_behind(value, axis, steps):
@@ -102,7 +115,7 @@
     floor_diag = jnp.maximum(jnp.abs(jnp.diagonal(own_block)), 1.0)
     current = guess
     for sweep in range(2):
-        gathered = lax.all_gather(current, "row", axis=0, tiled=True)
+        gathered = rates_start(current)
         applied = lax.psum_scatter(
             jnp.dot(matrix, gathered, precision=highest), "col", scatter_dimension=0, tiled=True
         )

time: 1120 us -> 1070 us (0.955)
  waiting for transfers between devices: 558 us -> 288 us
  blocking collectives: 0 us -> 257 us
  starting transfers between devices: 176 us -> 129 us
    all_to_all x0 -> x2, blocking collectives: none -> 257 us  [the longest x1 237 us: on_device(): lax.all_to_all(sent_blocks.reshape(dev_count, slot_cap, CB, CB), ('row',...]
    all_to_all x1, waiting for transfers between devices: 238 us -> 0.01 us  [map_views_on_mesh(): ready = jax.lax.all_to_all(formed, axis_tag, 0, 0)]
    all_to_all x1, starting transfers between devices: 50.5 us -> 3.56 us  [map_views_on_mesh(): ready = jax.lax.all_to_all(formed, axis_tag, 0, 0)]
    all_gather x2 -> x0, waiting for transfers between devices: 23.5 us -> none  [on_device(): gathered = lax.all_gather(current, 'row', axis=0, tiled=True)]
    unnamed x41 -> x39, local copies, waits for them, and re-layouts: 30 us -> 30.1 us
  transfers between devices with their start and end apart: 20 -> 18, of which waited for: 7 -> 5; matrix products, arithmetic and copies ran while one was open for 30% -> 32% of each run, Pallas kernels for 0% -> 0%
where the time goes in v1:
time: 1070 us; the launch traced here: 1060 us
  waiting for transfers between devices  288 us (27%)
  blocking collectives  257 us (24%)
  local copies, waits for them, and re-layouts  165 us (15%)
  starting transfers between devices  129 us (12%)
  other arithmetic  114 us (11%)
  matrix products  87.3 us (8%)
  between operations  14.6 us (1%)
    all_to_all x1, blocking collectives, on_device(): lax.all_to_all(sent_blocks.reshape(dev_count, slot_cap, CB, CB), ('row',...  237 us
    ppermute x14, waiting for transfers between devices, from_behind(): return lax.ppermute(value, axis, pairs)  148 us
    reduce_scatter x2, waiting for transfers between devices, on_device(): lax.psum_scatter(jnp.dot(matrix, gathered, precision=highest), 'col', sca...  140 us
    ppermute x14, starting transfers between devices, from_behind(): return lax.ppermute(value, axis, pairs)  117 us
    scatter-add x1, other arithmetic, on_device(): jax.ops.segment_sum(got_blocks.reshape(-1, CB, CB), places, num_segments=...  52 us
    scatter-add x1, other arithmetic, on_device(): jax.ops.segment_sum(partial_value, slot, num_segments=dev_count * slot_ca...  51.5 us
    reshape x2, local copies, waits for them, and re-layouts, on_device(): partial_value.reshape(local_rows, KA, KP, CB, KP, CB)  45.7 us
    dot_general x1, matrix products, on_device(): jnp.einsum('skab,skbn->skan', a_blocks, ghost_p, precision=highest)  43.2 us
  transfers between devices with their start and end apart: 18, of which 5 were waited for; matrix products, arithmetic and copies ran while one was open for 32% of the time, Pallas kernels for 0%

profile of v1, /device:TPU:0, one launch (start us, length us, event | category | flops | bytes accessed | tf_op | source)
XLA Modules:
  0.0 1055.1 jit_solution(14870073482332205015)
XLA Ops:
  7.2 1.2 fusion.9
  9.8 3.4 collective-permute-start.1
  15.0 3.6 collective-permute-start.2
  18.6 2.9 reshape.351
  21.5 2.0 gather_fusion.8
  23.5 2.9 copy.130
  26.5 2.0 gather_fusion.7
  28.5 2.9 copy.129
  31.4 1.6 collective-permute-start.7
  34.1 4.1 copy.128
  38.2 2.1 gather_fusion.9
  40.8 2.0 gather_fusion.10
  43.3 2.0 gather_fusion.11
  45.9 2.0 gather_fusion.12
  48.5 2.0 gather_fusion.13
  50.5 4.1 reshape.502
  54.6 1.8 copy.131
  56.5 3.1 copy.132
  59.6 1.8 copy.133
  61.4 3.0 copy.134
  64.5 1.5 constant_dynamic-update-slice_fusion.8
  66.0 2.9 copy.135
  68.9 1.2 collective-permute-start.3
  70.2 2.7 collective-permute-start.4
  73.0 2.2 collective-permute-start.5
  75.2 47.5 %collective-permute-start.9 = (f32[8,256,256]{1,2,0:T(8,128)}, f32[8,256,256]{1,2,0:T(8,128)}, u32[]{:S(2)}, u32[]{:S(2)}) collective-permute-start(f32[8,256,256]{1,2,0:T(8,128)} %copy.131), channel_id=1, source_target_pairs={{0,3},{1,4},{2,5},{3,6},{4,7},{5,8},{6,9},{7,10},{8,11},{9,12},{10... | collective-permute-start | bytes 6291464 | tf_op jit(solution)/shard_map/ppermute | solution.py:30
  123.9 44.1 %collective-permute-done.6 = f32[8,2]{1,0:T(8,128)S(1)} collective-permute-done((f32[8,2]{1,0:T(8,128)S(1)}, f32[8,2]{1,0:T(8,128)S(1)}, u32[]{:S(2)}, u32[]{:S(2)}) %collective-permute-start.6) | collective-permute-done | bytes 96 | tf_op jit(solution)/shard_map/ppermute | solution.py:30
  168.4 47.2 %collective-permute-start.12 = (f32[8,256,256]{1,2,0:T(8,128)}, f32[8,256,256]{1,2,0:T(8,128)}, u32[]{:S(2)}, u32[]{:S(2)}) collective-permute-start(f32[8,256,256]{1,2,0:T(8,128)} %copy.134), channel_id=1, source_target_pairs={{0,6},{1,7},{2,8},{3,9},{4,10},{5,11},{6,12},{7,13},{8,14},{9,15},... | collective-permute-start | bytes 6291464 | tf_op jit(solution)/shard_map/ppermute | solution.py:30
  216.0 6.1 collective-permute-start.13
  222.2 2.3 scatter_custom_fusion
  225.3 7.6 all-to-all-start
  232.9 3.0 bitcast_dynamic-update-slice_fusion.6
  235.9 3.0 bitcast_dynamic-update-slice_fusion.5
  238.9 3.0 bitcast_dynamic-update-slice_fusion.4
  242.0 3.0 bitcast_dynamic-update-slice_fusion.3
  245.0 16.1 %collective-permute-done.11 = f32[8,256,256]{1,2,0:T(8,128)} collective-permute-done((f32[8,256,256]{1,2,0:T(8,128)}, f32[8,256,256]{1,2,0:T(8,128)}, u32[]{:S(2)}, u32[]{:S(2)}) %collective-permute-start.11) | collective-permute-done | bytes 2097184 | tf_op jit(solution)/shard_map/ppermute | solution.py:30
  261.1 3.0 bitcast_dynamic-update-slice_fusion.2
  264.1 88.1 %collective-permute-done.12 = f32[8,256,256]{1,2,0:T(8,128)} collective-permute-done((f32[8,256,256]{1,2,0:T(8,128)}, f32[8,256,256]{1,2,0:T(8,128)}, u32[]{:S(2)}, u32[]{:S(2)}) %collective-permute-start.12) | collective-permute-done | bytes 2097184 | tf_op jit(solution)/shard_map/ppermute | solution.py:30
  352.2 3.0 bitcast_dynamic-update-slice_fusion.1
  355.2 3.0 bitcast_dynamic-update-slice_fusion
  358.2 43.2 %multiply_bitcast_fusion = f32[8,8,256,256]{2,3,1,0:T(8,128)} fusion(f32[8,8,256,256]{2,3,1,0:T(8,128)} %bitcast_dynamic-update-slice_fusion, f32[8,8,256,256]{3,2,1,0:T(8,128)} %param.11, f32[8,8]{1,0:T(8,128)S(1)} %convert_element_type.80), kind=kOutput, calls=%fused_computation.18 | convolution fusion | flops 12889096192 | bytes 50331904 | tf_op jit(solution)/shard_map/skab,skbn->skan/dot_general | solution.py:59
  401.4 3.3 fusion
  404.7 21.4 %convolution_bitcast_fusion = f32[8,8,256,256]{2,3,1,0:T(8,128)} fusion(f32[8,8,256,256]{2,3,1,0:T(8,128)} %fusion, f32[8,256,256,1]{2,1,0,3:T(8,128)S(1)} %copy-done.3), kind=kOutput, calls=%fused_computation.19 | convolution fusion | flops 12884901888 | bytes 35651584 | tf_op jit(solution)/shard_map/sam,skan->skmn/dot_general | solution.py:62
  426.1 20.8 %reshape.352 = f32[8,8,2,128,2,128]{3,2,5,4,1,0:T(2,128)} reshape(f32[8,8,256,256]{2,3,1,0:T(8,128)} %convolution_bitcast_fusion) | data formatting | bytes 33554432 | tf_op jit(solution)/shard_map/reshape | solution.py:64
  446.9 25.0 %copy.136 = f32[8,8,2,128,2,128]{5,3,4,2,1,0:T(8,128)} copy(f32[8,8,2,128,2,128]{3,2,5,4,1,0:T(2,128)} %reshape.352) | data formatting | bytes 33554432 | tf_op jit(solution)/shard_map/reshape | solution.py:64
  471.8 7.9 broadcast_in_dim.27
  479.7 51.5 %scatter_fusion = f32[257,128,128]{2,1,0:T(8,128)} fusion(f32[257,128,128]{2,1,0:T(8,128)} %broadcast_in_dim.27, s32[256]{0:T(256)S(1)} %bitcast.88, f32[256,128,128]{2,1,0:T(8,128)} %bitcast.80), kind=kCustom, calls=%fused_computation.16 | custom fusion | flops 4194304 | bytes 50332672 | tf_op jit(solution)/shard_map/scatter-add | solution.py:81
  531.2 11.6 %slice.99 = f32[256,128,128]{2,1,0:T(8,128)} slice(f32[257,128,128]{2,1,0:T(8,128)} %scatter_fusion), slice={[0:256], [0:128], [0:128]} | slice | bytes 33554432 | tf_op jit(solution)/shard_map/slice | solution.py:81
  542.9 237.0 %all_to_all.24 = f32[128,2,128,128]{3,2,1,0:T(8,128)} all-to-all(f32[128,2,128,128]{3,2,1,0:T(8,128)} %bitcast.79), channel_id=1, replica_groups=mesh['row'=8,'col'=16] {'row','col'}, dimensions={0} | all-to-all | bytes 33554432 | tf_op jit(solution)/shard_map/all_to_all | solution.py:88
  779.8 1.1 stack.90
  781.0 3.6 all-to-all-start.2
  785.3 4.3 broadcast_in_dim.20
  789.6 52.0 %scatter_fusion.1 = f32[129,128,128]{2,1,0:T(8,128)} fusion(f32[129,128,128]{2,1,0:T(8,128)} %broadcast_in_dim.20, s32[256]{0:T(256)S(1)} %bitcast.89, f32[256,128,128]{2,1,0:T(8,128)} %bitcast.78), kind=kCustom, calls=%fused_computation.17 | custom fusion | flops 4194304 | bytes 50332672 | tf_op jit(solution)/shard_map/scatter-add | solution.py:105
  841.7 4.0 slice.100
  845.7 9.9 copy.137
  855.6 11.3 %fusion.20 = f32[2048,256]{1,0:T(8,128)} fusion(f32[1024,256]{1,0:T(8,128)S(1)} %bitcast.85, f32[256,8,8,128]{3,2,1,0:T(8,128)} %bitcast.74), kind=kOutput, calls=%fused_computation.105 | convolution fusion | flops 6442450944 | bytes 11534336 | tf_op jit(solution)/shard_map/dot_general | solution.py:120
  867.0 5.5 copy.145
  872.6 1.2 gather_fusion.14
  873.8 67.4 %reduce-scatter.3.cloned.1.call-done = f32[128,256]{1,0:T(8,128)} async-done(((f32[2048,256]{1,0:T(8,128)}), f32[128,256]{1,0:T(8,128)}) %reduce-scatter.3.cloned.1.call-update) | async-done | bytes 131088 | tf_op jit(solution)/shard_map/reduce_scatter | solution.py:119
  941.2 1.0 divide_add_fusion.1
  942.3 20.2 %all_to_all.25 = f32[8,128,256]{2,1,0:T(8,128)S(1)} all-to-all(f32[8,128,256]{2,1,0:T(8,128)S(1)} %stack.91), channel_id=1, replica_groups=mesh['row'=8,'col'=16] {'row'}, dimensions={0} | all-to-all | bytes 2097152 | tf_op jit(solution)/shard_map/all_to_all | solution.py:20
  962.5 11.2 %fusion.19 = f32[2048,256]{1,0:T(8,128)} fusion(f32[1024,256]{1,0:T(8,128)S(1)} %bitcast.86, f32[256,8,8,128]{3,2,1,0:T(8,128)} %bitcast.76), kind=kOutput, calls=%fused_computation.104 | convolution fusion | flops 6442450944 | bytes 11534336 | tf_op jit(solution)/shard_map/dot_general | solution.py:120
  973.8 72.6 %reduce-scatter.5.cloned.1.call-done = f32[128,256]{1,0:T(8,128)} async-done(((f32[2048,256]{1,0:T(8,128)}), f32[128,256]{1,0:T(8,128)}) %reduce-scatter.5.cloned.1.call-update) | async-done | bytes 131088 | tf_op jit(solution)/shard_map/reduce_scatter | solution.py:119
  1046.4 1.6 divide_add_fusion
  (110 shorter events, 10.5 us)
Async XLA Ops:
  7.2 25.8 %copy-start = (f32[16,256]{1,0:T(8,128)S(1)}, f32[16,256]{1,0:T(8,128)}, u32[]{:S(2)}) copy-start(f32[16,256]{1,0:T(8,128)} %param.17) | copy-start | bytes 49156
  9.8 59.1 %collective-permute-start.1 = (f32[8,2]{1,0:T(8,128)S(1)}, f32[8,2]{1,0:T(8,128)S(1)}, u32[]{:S(2)}, u32[]{:S(2)}) collective-permute-start(f32[8,2]{1,0:T(8,128)S(1)} %convert_element_type.65), channel_id=1, source_target_pairs={{0,2},{1,3},{2,4},{3,5},{4,6},{5,7},{6,8},{7,9},{8,10},{9,11},{10,... | collective-permute-start | bytes 200 | tf_op jit(solution)/shard_map/ppermute | solution.py:30
  13.7 56.5 %collective-permute-start = (f32[8,2]{1,0:T(8,128)S(1)}, f32[8,2]{1,0:T(8,128)S(1)}, u32[]{:S(2)}, u32[]{:S(2)}) collective-permute-start(f32[8,2]{1,0:T(8,128)S(1)} %convert_element_type.63), channel_id=1, source_target_pairs={{0,1},{1,2},{2,3},{3,4},{4,5},{5,6},{6,7},{7,8},{8,9},{9,10},{10,1... | collective-permute-start | bytes 200 | tf_op jit(solution)/shard_map/ppermute | solution.py:30
  15.0 57.9 %collective-permute-start.2 = (f32[8,2]{1,0:T(8,128)S(1)}, f32[8,2]{1,0:T(8,128)S(1)}, u32[]{:S(2)}, u32[]{:S(2)}) collective-permute-start(f32[8,2]{1,0:T(8,128)S(1)} %convert_element_type.67), channel_id=1, source_target_pairs={{0,3},{1,4},{2,5},{3,6},{4,7},{5,8},{6,9},{7,10},{8,11},{9,12},{10... | collective-permute-start | bytes 200 | tf_op jit(solution)/shard_map/ppermute | solution.py:30
  26.4 142.0 %collective-permute-start.8 = (f32[8,256,256]{1,2,0:T(8,128)}, f32[8,256,256]{1,2,0:T(8,128)}, u32[]{:S(2)}, u32[]{:S(2)}) collective-permute-start(f32[8,256,256]{1,2,0:T(8,128)} %copy.130), channel_id=1, source_target_pairs={{0,2},{1,3},{2,4},{3,5},{4,6},{5,7},{6,8},{7,9},{8,10},{9,11},{10,... | collective-permute-start | bytes 6291464 | tf_op jit(solution)/shard_map/ppermute | solution.py:30
  28.5 4.5 copy-start.9
  28.5 4.5 copy-start.8
  28.5 4.5 copy-start.10
  31.4 184.6 %collective-permute-start.7 = (f32[8,256,256]{1,2,0:T(8,128)}, f32[8,256,256]{1,2,0:T(8,128)}, u32[]{:S(2)}, u32[]{:S(2)}) collective-permute-start(f32[8,256,256]{1,2,0:T(8,128)} %copy.129), channel_id=1, source_target_pairs={{0,1},{1,2},{2,3},{3,4},{4,5},{5,6},{6,7},{7,8},{8,9},{9,10},{10,1... | collective-permute-start | bytes 6291464 | tf_op jit(solution)/shard_map/ppermute | solution.py:30
  50.5 4.1 copy-start.4
  56.5 3.1 copy-start.5
  61.4 3.0 copy-start.2
  68.9 6.4 collective-permute-start.3
  70.2 52.7 %collective-permute-start.4 = (f32[8,2]{1,0:T(8,128)S(1)}, f32[8,2]{1,0:T(8,128)S(1)}, u32[]{:S(2)}, u32[]{:S(2)}) collective-permute-start(f32[8,2]{1,0:T(8,128)S(1)} %convert_element_type.71), channel_id=1, source_target_pairs={{0,5},{1,6},{2,7},{3,8},{4,9},{5,10},{6,11},{7,12},{8,13},{9,14},{... | collective-permute-start | bytes 200 | tf_op jit(solution)/shard_map/ppermute | solution.py:30
  73.0 50.2 %collective-permute-start.5 = (f32[8,2]{1,0:T(8,128)S(1)}, f32[8,2]{1,0:T(8,128)S(1)}, u32[]{:S(2)}, u32[]{:S(2)}) collective-permute-start(f32[8,2]{1,0:T(8,128)S(1)} %convert_element_type.73), channel_id=1, source_target_pairs={{0,6},{1,7},{2,8},{3,9},{4,10},{5,11},{6,12},{7,13},{8,14},{9,15},... | collective-permute-start | bytes 200 | tf_op jit(solution)/shard_map/ppermute | solution.py:30
  75.2 163.7 %collective-permute-start.9 = (f32[8,256,256]{1,2,0:T(8,128)}, f32[8,256,256]{1,2,0:T(8,128)}, u32[]{:S(2)}, u32[]{:S(2)}) collective-permute-start(f32[8,256,256]{1,2,0:T(8,128)} %copy.131), channel_id=1, source_target_pairs={{0,3},{1,4},{2,5},{3,6},{4,7},{5,8},{6,9},{7,10},{8,11},{9,12},{10... | collective-permute-start | bytes 6291464 | tf_op jit(solution)/shard_map/ppermute | solution.py:30
  122.9 119.1 %collective-permute-start.10 = (f32[8,256,256]{1,2,0:T(8,128)}, f32[8,256,256]{1,2,0:T(8,128)}, u32[]{:S(2)}, u32[]{:S(2)}) collective-permute-start(f32[8,256,256]{1,2,0:T(8,128)} %copy.132), channel_id=1, source_target_pairs={{0,4},{1,5},{2,6},{3,7},{4,8},{5,9},{6,10},{7,11},{8,12},{9,13},{1... | collective-permute-start | bytes 6291464 | tf_op jit(solution)/shard_map/ppermute | solution.py:30
  123.2 44.8 %collective-permute-start.6 = (f32[8,2]{1,0:T(8,128)S(1)}, f32[8,2]{1,0:T(8,128)S(1)}, u32[]{:S(2)}, u32[]{:S(2)}) collective-permute-start(f32[8,2]{1,0:T(8,128)S(1)} %convert_element_type.75), channel_id=1, source_target_pairs={{0,7},{1,8},{2,9},{3,10},{4,11},{5,12},{6,13},{7,14},{8,15},{9,0},... | collective-permute-start | bytes 200 | tf_op jit(solution)/shard_map/ppermute | solution.py:30
  168.0 93.1 %collective-permute-start.11 = (f32[8,256,256]{1,2,0:T(8,128)}, f32[8,256,256]{1,2,0:T(8,128)}, u32[]{:S(2)}, u32[]{:S(2)}) collective-permute-start(f32[8,256,256]{1,2,0:T(8,128)} %copy.133), channel_id=1, source_target_pairs={{0,5},{1,6},{2,7},{3,8},{4,9},{5,10},{6,11},{7,12},{8,13},{9,14},{... | collective-permute-start | bytes 6291464 | tf_op jit(solution)/shard_map/ppermute | solution.py:30
  168.4 183.7 %collective-permute-start.12 = (f32[8,256,256]{1,2,0:T(8,128)}, f32[8,256,256]{1,2,0:T(8,128)}, u32[]{:S(2)}, u32[]{:S(2)}) collective-permute-start(f32[8,256,256]{1,2,0:T(8,128)} %copy.134), channel_id=1, source_target_pairs={{0,6},{1,7},{2,8},{3,9},{4,10},{5,11},{6,12},{7,13},{8,14},{9,15},... | collective-permute-start | bytes 6291464 | tf_op jit(solution)/shard_map/ppermute | solution.py:30
  216.0 139.2 %collective-permute-start.13 = (f32[8,256,256]{1,2,0:T(8,128)}, f32[8,256,256]{1,2,0:T(8,128)}, u32[]{:S(2)}, u32[]{:S(2)}) collective-permute-start(f32[8,256,256]{1,2,0:T(8,128)} %copy.135), channel_id=1, source_target_pairs={{0,7},{1,8},{2,9},{3,10},{4,11},{5,12},{6,13},{7,14},{8,15},{9,0},... | collective-permute-start | bytes 6291464 | tf_op jit(solution)/shard_map/ppermute | solution.py:30
  225.3 317.6 %all-to-all-start = ((f32[128,1,2]{2,1,0:T(1,128)}), f32[128,1,2]{2,1,0:T(1,128)S(1)}, u32[]{:S(2)}, u32[]{:S(2)}) async-start(f32[128,1,2]{2,1,0:T(1,128)} %bitcast.10), calls=%async_computation | async-start | bytes 131072 | tf_op jit(solution)/shard_map/all_to_all | solution.py:95
  401.4 3.3 copy-start.3
  542.9 237.0 %copy-start.6 = (f32[128,256]{1,0:T(8,128)S(1)}, f32[128,256]{1,0:T(8,128)}, u32[]{:S(2)}) copy-start(f32[128,256]{1,0:T(8,128)} %param.19) | copy-start | bytes 393220
  781.0 74.6 %all-to-all-start.2 = ((f32[8,128,256]{2,1,0:T(8,128)}), f32[8,128,256]{2,1,0:T(8,128)S(1)}, u32[]{:S(2)}, u32[]{:S(2)}) async-start(f32[8,128,256]{2,1,0:T(8,128)} %stack.90), calls=%async_computation.2 | async-start | bytes 2097152 | tf_op jit(solution)/shard_map/all_to_all | solution.py:20
  784.5 156.7 %reduce-scatter.3.cloned.1.call-start = ((), (), s32[]{:S(2)}) async-start(), calls=%async_computation.6 | async-start | bytes 2228224 | tf_op jit(solution)/shard_map/reduce_scatter | solution.py:119
  867.0 179.4 %reduce-scatter.5.cloned.1.call-start = ((), (), s32[]{:S(2)}) async-start(), calls=%async_computation.7 | async-start | bytes 2228224 | tf_op jit(solution)/shard_map/reduce_scatter | solution.py:119
  867.0 74.2 %copy-start.7 = (f32[128,256]{1,0:T(8,128)S(1)}, f32[128,256]{1,0:T(8,128)}, u32[]{:S(2)}) copy-start(f32[128,256]{1,0:T(8,128)} %param.18) | copy-start | bytes 393220
  962.5 85.5 %copy-start.1 = (f32[16,256]{1,0:T(8,128)S(1)}, f32[16,256]{1,0:T(8,128)}, u32[]{:S(2)}) copy-start(f32[16,256]{1,0:T(8,128)} %param.17) | copy-start | bytes 49156
Sparse Core Ops, SparseCore 0:
  867.1 74.1 reduce-scatter.2
  973.9 72.4 reduce-scatter.4
